TPU v7x, 32 devices: a whole 2x2x4 slice. The times are simulated.
32 devices in a mesh: grp: 2 (over y), samp: 4 (over z), snp: 4 (over x, core).
Axes of the slice: x: 2, y: 2, z: 4, core: 2. Of those that a mesh axis runs over, the one named last changes fastest.
Arguments:
- genotypes: int32 [2048, 8192], P(('grp', 'samp'), 'snp'), parts along dimension 0, may hold values from 0 to 2730, as said below
- basis_cols: bfloat16 [16384, 256], P(('grp', 'snp')), parts along dimension 0, may hold values from -0.0625 to 0.0625
Outputs:
- y_block: float32 [8, 4, 512, 256], P(('grp', 'snp'), 'samp'), parts along dimension 0
- r_factor: float32 [512, 256], P('grp'), parts along dimension 0
- q_next: float32 [8, 4, 512, 256], P(('grp', 'snp'), 'samp'), parts along dimension 0
There are 2 independent parts, one for each index of `grp`. A program takes and returns all parts, laid end to end along the dimension named above; each array names one. Nothing has to cross between parts.
Inputs may be any that keep to these rules, and one draw needn't show every extreme that they name: `genotypes`: each word packs 6 dosages of 0, 1 or 2 in pairs of bits: bits 2 t and 2 t + 1 of word (w, p) hold the dosage of sample 6 w + t at SNP p, t from 0 to 5; bits 12 and up are zero.
All inputs are finite; a program needn't handle non-finite values.
Results may differ from a plain program's by a relative error of at most 0.0025.
Values may be sent and summed in bfloat16 or wider, within the bound.
A program may use at most 64 MiB of HBM per device.

v0:
```python
import jax
import jax.numpy as jnp
from jax import lax
from jax.sharding import PartitionSpec as P


def unpack_counts(genotypes):
    planes = [
        jnp.bitwise_and(jnp.right_shift(genotypes, 2 * shift_pos), 3) for shift_pos in range(6)
    ]
    local_counts = planes[0].sum(axis=0)
    for plane_item in planes[1:]:
        local_counts = local_counts + plane_item.sum(axis=0)
    dosage = jnp.stack([plane_item.astype(jnp.bfloat16) for plane_item in planes], axis=1)
    dosage = dosage.reshape(genotypes.shape[0] * 6, genotypes.shape[1])
    return (dosage, local_counts)


def per_device(genotypes, basis_cols):
    dosage, local_counts = unpack_counts(genotypes)
    sample_rows, snp_cols = dosage.shape
    width = basis_cols.shape[1]
    totals = lax.psum(local_counts, "samp")
    samples = sample_rows * lax.axis_size("samp")
    allele_mean = totals.astype(jnp.float32) / jnp.float32(samples)
    center = jnp.dot(allele_mean, basis_cols.astype(jnp.float32), precision=lax.Precision.HIGHEST)
    inv_root = jnp.float32(1.0) / jnp.sqrt(jnp.float32(samples))
    contract_rows = (((0,), (0,)), ((), ()))
    product_term = jnp.dot(dosage, basis_cols, preferred_element_type=jnp.float32) - center[None, :]
    score_rows = lax.psum(product_term, "snp").astype(jnp.bfloat16)
    y_local = lax.psum_scatter(
        lax.dot_general(dosage, score_rows, contract_rows, preferred_element_type=jnp.float32)
        * inv_root,
        "samp",
        scatter_dimension=0,
        tiled=True,
    )
    snp_total = snp_cols * lax.axis_size("snp")
    local_gram = jnp.dot(y_local.T, y_local, precision=lax.Precision.HIGHEST) / jnp.float32(
        snp_total
    )
    gram_sum = lax.psum(local_gram, ("samp", "snp"))
    lower_factor = jnp.linalg.cholesky(gram_sum)
    q_next = lax.linalg.triangular_solve(
        lower_factor, y_local, left_side=False, lower=True, transpose_a=True
    )
    layout = (1, 1, y_local.shape[0], width)
    return (y_local.reshape(layout), lower_factor.T, q_next.reshape(layout))


def solution(mesh):
    return jax.shard_map(
        per_device,
        mesh=mesh,
        in_specs=(P(("grp", "samp"), "snp"), P(("grp", "snp"), None)),
        out_specs=(
            P(("grp", "snp"), "samp", None, None),
            P("grp", None),
            P(("grp", "snp"), "samp", None, None),
        ),
        check_vma=False,
    )
```

profile of v0, /device:TPU:0, one launch (start us, length us, event | category | flops | bytes accessed | tf_op | source)
XLA Modules:
  0.0 291.1 jit_solution(1570081549035918999)
XLA Ops:
  7.2 0.0 copy-start
  7.2 0.0 copy-start.1
  7.2 0.0 reduce-scatter.2.cloned.1.call-start
  7.2 2.0 fusion.23
  9.2 0.3 copy-done.1
  9.5 1.2 fusion.2
  10.7 0.3 fusion.21
  11.0 0.3 fusion.19
  11.3 0.3 fusion.17
  11.5 0.3 fusion.15
  11.8 0.3 fusion.13
  12.1 6.9 %copy.9 = bf16[256,6,2048]{2,1,0:T(8,128)(2,1)} copy(bf16[256,6,2048]{2,0,1:T(8,128)(2,1)S(1)} %fusion.13) | data formatting | bytes 12582912 | tf_op jit(solution)/shard_map/stack | solution.py:14
  18.9 11.1 %reshape.33 = bf16[1536,2048]{1,0:T(8,128)(2,1)} reshape(bf16[256,6,2048]{2,1,0:T(8,128)(2,1)} %copy.9) | data formatting | bytes 12582912 | tf_op jit(solution)/shard_map/reshape | solution.py:15
  30.0 10.0 %psum.21 = s32[2048]{0:T(1024)S(1)} all-reduce(s32[2048]{0:T(1024)S(1)} %add_add_fusion), channel_id=1, replica_groups=mesh['grp'=2,'samp'=4,'snp'=4] {'samp'}, use_global_device_ids=true, to_apply=%region_6.0 | all-reduce | flops 2048 | bytes 16384 | tf_op jit(solution)/shard_map/psum | solution.py:23
  40.1 0.0 copy-done
  40.1 0.5 fusion.36
  40.6 4.6 %convolution_subtract_fusion = f32[1536,256]{1,0:T(8,128)S(1)} fusion(bf16[1536,2048]{1,0:T(8,128)(2,1)} %reshape.33, bf16[2048,256]{1,0:T(8,128)(2,1)S(1)} %copy-done, f32[256]{0:T(256)S(1)} %bitcast.72), kind=kOutput, calls=%fused_computation.3 | convolution fusion | flops 1611005952 | bytes 8913920 | tf_op jit(solution)/shard_map/dot_general | solution.py:29
  45.2 32.6 %all-reduce.5 = bf16[1536,256]{1,0:T(8,128)(2,1)S(1)} all-reduce(f32[1536,256]{1,0:T(8,128)S(1)} %convolution_subtract_fusion), channel_id=1, replica_groups=mesh['grp'=2,'samp'=4,'snp'=4] {'snp'}, use_global_device_ids=true, to_apply=%region_7.0 | all-reduce | flops 393216 | bytes 2359296 | tf_op jit(solution)/shard_map/psum | solution.py:30
  77.8 6.0 %convolution_multiply_fusion = f32[2048,256]{1,0:T(8,128)} fusion(bf16[1536,2048]{1,0:T(8,128)(2,1)} %reshape.33, bf16[1536,256]{1,0:T(8,128)(2,1)S(1)} %all-reduce.5), kind=kOutput, calls=%fused_computation.2 | convolution fusion | flops 1611137024 | bytes 9175040 | tf_op jit(solution)/shard_map/dot_general | solution.py:32
  83.8 0.0 reduce-scatter.2.cloned.1.call-update
  83.9 0.0 all-reduce.4.cloned.1.call-start
  83.9 42.3 %reduce-scatter.2.cloned.1.call-done = f32[512,256]{1,0:T(8,128)} async-done(((f32[2048,256]{1,0:T(8,128)}), f32[512,256]{1,0:T(8,128)}) %reduce-scatter.2.cloned.1.call-update) | async-done | bytes 524304 | tf_op jit(solution)/shard_map/reduce_scatter | solution.py:31
  126.2 2.9 convolution_multiply_fusion.1
  129.1 0.0 all-reduce.4.cloned.1.call-update
  129.2 90.0 %all-reduce.4.cloned.1.call-done = f32[256,256]{0,1:T(8,128)} async-done(((f32[256,256]{0,1:T(8,128)}), f32[256,256]{0,1:T(8,128)}) %all-reduce.4.cloned.1.call-update) | async-done | bytes 262160 | tf_op jit(solution)/shard_map/psum | solution.py:42
  219.2 1.1 copy.11
  220.2 0.0 copy-start.2
  220.3 1.0 fusion.27
  221.3 11.7 %cholesky.50 = f32[128,128]{1,0:T(8,128)S(1)} custom-call(f32[128,128]{1,0:T(8,128)S(1)} %cholesky.118), custom_call_target="Cholesky" | custom-call | tf_op jit(solution)/shard_map/jit(cholesky)/cholesky | solution.py:43
  233.1 9.8 %custom-call.14 = f32[1,128,128]{1,2,0:T(8,128)S(1)} custom-call(f32[1,128,128]{2,1,0:T(8,128)S(1)} %get-tuple-element.38), custom_call_target="InvertDiagBlocksLowerTriangular" | custom-call | tf_op jit(solution)/shard_map/jit(cholesky)/cholesky | solution.py:43
  242.9 0.2 constant_dynamic-update-slice_fusion.1
  243.1 0.3 convolution_subtract_fusion.2
  243.4 11.7 %cholesky.105 = f32[128,128]{1,0:T(8,128)S(1)} custom-call(f32[128,128]{1,0:T(8,128)S(1)} %convolution_subtract_fusion.2), custom_call_target="Cholesky" | custom-call | tf_op jit(solution)/shard_map/jit(cholesky)/cholesky | solution.py:43
  255.1 0.6 compare_reduce_fusion
  257.1 0.8 copy.12
  258.0 0.1 triangular_solve.43
  258.0 4.1 %while.1 = (s32[]{:T(128)}, f32[256,256]{1,0:T(8,128)S(1)}, s32[2,2]{1,0:T(2,128)S(1)}, f32[2,128,128]{2,1,0:T(8,128)S(1)}, s32[]{:T(128)}) while((s32[]{:T(128)}, f32[256,256]{1,0:T(8,128)S(1)}, s32[2,2]{1,0:T(2,128)S(1)}, f32[2,128,128]{2,1,0:T(8,128)S(1)}, s32[]{:T(128)}) %tuple.35), condition=%wide.while_cond, body=%wide.while_body.sunk | while | flops 2 | bytes 131189 | solution.py:44
  258.0 0.6 fusion.50
  258.6 1.4 bitcast_dynamic-update-slice_fusion.2
  260.1 0.6 fusion.50
  260.7 1.4 bitcast_dynamic-update-slice_fusion.2
  262.1 19.7 %custom-call.15 = f32[2,128,128]{1,2,0:T(8,128)S(1)} custom-call(f32[2,128,128]{2,1,0:T(8,128)S(1)} %get-tuple-element.10), custom_call_target="InvertDiagBlocksLowerTriangular" | custom-call | tf_op jit(solution)/shard_map/triangular_solve | solution.py:44
  281.8 0.0 copy-done.2
  281.8 0.4 fusion.25
  282.2 0.6 convolution_subtract_fusion.1
  282.8 0.4 fusion.30
  283.3 1.0 copy.13
  (12 shorter events, 0.2 us)
Async XLA Ops:
  7.2 32.9 %copy-start = (bf16[2048,256]{1,0:T(8,128)(2,1)S(1)}, bf16[2048,256]{1,0:T(8,128)(2,1)}, u32[]{:S(2)}) copy-start(bf16[2048,256]{1,0:T(8,128)(2,1)} %param.3) | copy-start | bytes 3145732
  7.2 2.3 copy-start.1
  7.2 119.0 %reduce-scatter.2.cloned.1.call-start = ((), (), s32[]{:S(2)}) async-start(), calls=%async_computation.1 | async-start | bytes 2621440 | tf_op jit(solution)/shard_map/reduce_scatter | solution.py:31
  83.9 135.3 %all-reduce.4.cloned.1.call-start = ((), (), s32[]{:S(2)}) async-start(), calls=%async_computation.2 | async-start | bytes 524288 | tf_op jit(solution)/shard_map/psum | solution.py:42
  220.2 61.6 %copy-start.2 = (f32[512,256]{1,0:T(8,128)S(1)}, f32[512,256]{1,0:T(8,128)}, u32[]{:S(2)}) copy-start(f32[512,256]{1,0:T(8,128)} %reduce-scatter.2.cloned.1.call-done) | copy-start | bytes 1572868
Sparse Core Ops, SparseCore 0:
  84.0 42.1 reduce-scatter.1
  130.2 88.9 all-reduce.3
where the time goes:
time: 292 us; the launch traced here: 291 us
  waiting for transfers between devices  132 us (45%)
  other arithmetic  59.3 us (20%)
  blocking collectives  42.7 us (15%)
  local copies, waits for them, and re-layouts  25.3 us (9%)
  matrix products  15.9 us (5%)
  between operations  15.6 us (5%)
    psum x1, waiting for transfers between devices, per_device(): gram_sum = lax.psum(local_gram, ('samp', 'snp'))  90 us
    reduce_scatter x1, waiting for transfers between devices, per_device(): lax.psum_scatter(lax.dot_general(dosage, score_rows, contract_rows, prefe...  42.3 us
    another operation x6, other arithmetic, per_device(): lower_factor = jnp.linalg.cholesky(gram_sum)  33.9 us
    psum x1, blocking collectives, per_device(): score_rows = lax.psum(product_term, 'snp').astype(jnp.bfloat16)  32.6 us
    another operation x3, other arithmetic, per_device(): lax.linalg.triangular_solve(lower_factor, y_local, left_side=False, lower...  19.7 us
    reshape x1, local copies, waits for them, and re-layouts, unpack_counts(): dosage = dosage.reshape(genotypes.shape[0] * 6, genotypes.shape[1])  11.1 us
    psum x1, blocking collectives, per_device(): totals = lax.psum(local_counts, 'samp')  10 us
    another operation x1, local copies, waits for them, and re-layouts, unpack_counts(): jnp.stack([plane_item.astype(jnp.bfloat16) for plane_item in planes], axi...  6.86 us
  transfers between devices with their start and end apart: 2, of which 2 were waited for; matrix products, arithmetic and copies ran while one was open for 0% of the time, Pallas kernels for 0%

commit v1 on v0

--- a/solution.py
+++ b/solution.py
@@ -39,7 +39,7 @@
     local_gram = jnp.dot(y_local.T, y_local, precision=lax.Precision.HIGHEST) / jnp.float32(
         snp_total
     )
-    gram_sum = lax.psum(local_gram, ("samp", "snp"))
+    gram_sum = jnp.sum(lax.all_gather(local_gram, ("samp", "snp")), axis=0)
     lower_factor = jnp.linalg.cholesky(gram_sum)
     q_next = lax.linalg.triangular_solve(
         lower_factor, y_local, left_side=False, lower=True, transpose_a=True

time: 292 us -> 252 us (0.86)
  waiting for transfers between devices: 132 us -> 92 us
    psum x1 -> x0, waiting for transfers between devices: 90 us -> none  [per_device(): gram_sum = lax.psum(local_gram, ('samp', 'snp'))]
    all_gather x0 -> x1, waiting for transfers between devices: none -> 49.7 us  [per_device(): gram_sum = jnp.sum(lax.all_gather(local_gram, ('samp', 'snp')), axis=0)]
where the time goes in v1:
time: 252 us; the launch traced here: 251 us
  waiting for transfers between devices  92 us (37%)
  other arithmetic  60.8 us (24%)
  blocking collectives  42.7 us (17%)
  local copies, waits for them, and re-layouts  24.3 us (10%)
  matrix products  16 us (6%)
  between operations  15.6 us (6%)
    all_gather x1, waiting for transfers between devices, per_device(): gram_sum = jnp.sum(lax.all_gather(local_gram, ('samp', 'snp')), axis=0)  49.7 us
    reduce_scatter x1, waiting for transfers between devices, per_device(): lax.psum_scatter(lax.dot_general(dosage, score_rows, contract_rows, prefe...  42.3 us
    another operation x6, other arithmetic, per_device(): lower_factor = jnp.linalg.cholesky(gram_sum)  33.9 us
    psum x1, blocking collectives, per_device(): score_rows = lax.psum(product_term, 'snp').astype(jnp.bfloat16)  32.6 us
    another operation x3, other arithmetic, per_device(): lax.linalg.triangular_solve(lower_factor, y_local, left_side=False, lower...  19.7 us
    reshape x1, local copies, waits for them, and re-layouts, unpack_counts(): dosage = dosage.reshape(genotypes.shape[0] * 6, genotypes.shape[1])  11.1 us
    psum x1, blocking collectives, per_device(): totals = lax.psum(local_counts, 'samp')  10 us
    another operation x1, local copies, waits for them, and re-layouts, unpack_counts(): jnp.stack([plane_item.astype(jnp.bfloat16) for plane_item in planes], axi...  6.86 us
  transfers between devices with their start and end apart: 2, of which 2 were waited for; matrix products, arithmetic and copies ran while one was open for 0% of the time, Pallas kernels for 0%

profile of v1, /device:TPU:0, one launch (start us, length us, event | category | flops | bytes accessed | tf_op | source)
XLA Modules:
  0.0 251.4 jit_solution(15746400675109472889)
XLA Ops:
  7.2 0.0 copy-start
  7.2 0.0 copy-start.1
  7.2 0.0 reduce-scatter.2.cloned.1.call-start
  7.2 2.0 fusion.23
  9.2 0.3 copy-done.1
  9.5 1.2 fusion.2
  10.7 0.3 fusion.21
  11.0 0.3 fusion.19
  11.3 0.3 fusion.17
  11.5 0.3 fusion.15
  11.8 0.3 fusion.13
  12.1 6.9 %copy.12 = bf16[256,6,2048]{2,1,0:T(8,128)(2,1)} copy(bf16[256,6,2048]{2,0,1:T(8,128)(2,1)S(1)} %fusion.13) | data formatting | bytes 12582912 | tf_op jit(solution)/shard_map/stack | solution.py:14
  18.9 11.1 %reshape.33 = bf16[1536,2048]{1,0:T(8,128)(2,1)} reshape(bf16[256,6,2048]{2,1,0:T(8,128)(2,1)} %copy.12) | data formatting | bytes 12582912 | tf_op jit(solution)/shard_map/reshape | solution.py:15
  30.0 10.0 %psum.14 = s32[2048]{0:T(1024)S(1)} all-reduce(s32[2048]{0:T(1024)S(1)} %add_add_fusion), channel_id=1, replica_groups=mesh['grp'=2,'samp'=4,'snp'=4] {'samp'}, use_global_device_ids=true, to_apply=%region_6.0 | all-reduce | flops 2048 | bytes 16384 | tf_op jit(solution)/shard_map/psum | solution.py:23
  40.1 0.0 copy-done
  40.1 0.5 fusion.36
  40.6 4.6 %convolution_subtract_fusion = f32[1536,256]{1,0:T(8,128)S(1)} fusion(bf16[1536,2048]{1,0:T(8,128)(2,1)} %reshape.33, bf16[2048,256]{1,0:T(8,128)(2,1)S(1)} %copy-done, f32[256]{0:T(256)S(1)} %bitcast.74), kind=kOutput, calls=%fused_computation.3 | convolution fusion | flops 1611005952 | bytes 8913920 | tf_op jit(solution)/shard_map/dot_general | solution.py:29
  45.2 32.6 %all-reduce.2 = bf16[1536,256]{1,0:T(8,128)(2,1)S(1)} all-reduce(f32[1536,256]{1,0:T(8,128)S(1)} %convolution_subtract_fusion), channel_id=1, replica_groups=mesh['grp'=2,'samp'=4,'snp'=4] {'snp'}, use_global_device_ids=true, to_apply=%region_7.0 | all-reduce | flops 393216 | bytes 2359296 | tf_op jit(solution)/shard_map/psum | solution.py:30
  77.8 6.0 %convolution_multiply_fusion = f32[2048,256]{1,0:T(8,128)} fusion(bf16[1536,2048]{1,0:T(8,128)(2,1)} %reshape.33, bf16[1536,256]{1,0:T(8,128)(2,1)S(1)} %all-reduce.2), kind=kOutput, calls=%fused_computation.2 | convolution fusion | flops 1611137024 | bytes 9175040 | tf_op jit(solution)/shard_map/dot_general | solution.py:32
  83.8 0.0 reduce-scatter.2.cloned.1.call-update
  83.9 0.0 all-gather.3.cloned.1.call-start
  83.9 42.3 %reduce-scatter.2.cloned.1.call-done = f32[512,256]{1,0:T(8,128)} async-done(((f32[2048,256]{1,0:T(8,128)}), f32[512,256]{1,0:T(8,128)}) %reduce-scatter.2.cloned.1.call-update) | async-done | bytes 524304 | tf_op jit(solution)/shard_map/reduce_scatter | solution.py:31
  126.2 2.9 %convolution_multiply_fusion.1 = f32[256,256]{1,0:T(8,128)} fusion(f32[512,256]{1,0:T(8,128)} %reduce-scatter.2.cloned.1.call-done), kind=kOutput, calls=%fused_computation.23 | convolution fusion | flops 402718720 | bytes 786432 | tf_op jit(solution)/shard_map/dot_general | solution.py:39
  129.1 0.0 all-gather.3.cloned.1.call-update
  129.2 49.7 %all-gather.3.cloned.1.call-done = f32[4096,256]{1,0:T(8,128)} async-done(((f32[256,256]{1,0:T(8,128)}), f32[4096,256]{1,0:T(8,128)}) %all-gather.3.cloned.1.call-update) | async-done | bytes 4194320 | tf_op jit(solution)/shard_map/all_gather | solution.py:42
  178.9 2.5 reduce_sum.69
  181.4 0.1 copy.13
  181.5 0.0 copy-start.2
  181.6 11.7 %cholesky.50 = f32[128,128]{1,0:T(8,128)S(1)} custom-call(f32[128,128]{1,0:T(8,128)S(1)} %cholesky.118), custom_call_target="Cholesky" | custom-call | tf_op jit(solution)/shard_map/jit(cholesky)/cholesky | solution.py:43
  193.3 9.8 %custom-call.14 = f32[1,128,128]{1,2,0:T(8,128)S(1)} custom-call(f32[1,128,128]{2,1,0:T(8,128)S(1)} %get-tuple-element.41), custom_call_target="InvertDiagBlocksLowerTriangular" | custom-call | tf_op jit(solution)/shard_map/jit(cholesky)/cholesky | solution.py:43
  203.1 0.2 constant_dynamic-update-slice_fusion.1
  203.4 0.3 convolution_subtract_fusion.2
  203.6 11.7 %cholesky.105 = f32[128,128]{1,0:T(8,128)S(1)} custom-call(f32[128,128]{1,0:T(8,128)S(1)} %convolution_subtract_fusion.2), custom_call_target="Cholesky" | custom-call | tf_op jit(solution)/shard_map/jit(cholesky)/cholesky | solution.py:43
  215.4 0.6 compare_reduce_fusion
  217.4 0.8 copy.14
  218.2 0.1 triangular_solve.43
  218.3 4.1 %while.1 = (s32[]{:T(128)}, f32[256,256]{1,0:T(8,128)S(1)}, s32[2,2]{1,0:T(2,128)S(1)}, f32[2,128,128]{2,1,0:T(8,128)S(1)}, s32[]{:T(128)}) while((s32[]{:T(128)}, f32[256,256]{1,0:T(8,128)S(1)}, s32[2,2]{1,0:T(2,128)S(1)}, f32[2,128,128]{2,1,0:T(8,128)S(1)}, s32[]{:T(128)}) %tuple.36), condition=%wide.while_cond, body=%wide.while_body.sunk | while | flops 2 | bytes 131189 | solution.py:44
  218.3 0.6 fusion.50
  218.9 1.4 bitcast_dynamic-update-slice_fusion.2
  220.3 0.6 fusion.50
  220.9 1.4 bitcast_dynamic-update-slice_fusion.2
  222.4 19.7 %custom-call.15 = f32[2,128,128]{1,2,0:T(8,128)S(1)} custom-call(f32[2,128,128]{2,1,0:T(8,128)S(1)} %get-tuple-element.10), custom_call_target="InvertDiagBlocksLowerTriangular" | custom-call | tf_op jit(solution)/shard_map/triangular_solve | solution.py:44
  242.1 0.0 copy-done.2
  242.1 0.4 fusion.25
  242.5 0.6 convolution_subtract_fusion.1
  243.1 0.4 fusion.30
  243.6 1.0 copy.15
  (13 shorter events, 0.2 us)
Async XLA Ops:
  7.2 32.9 %copy-start = (bf16[2048,256]{1,0:T(8,128)(2,1)S(1)}, bf16[2048,256]{1,0:T(8,128)(2,1)}, u32[]{:S(2)}) copy-start(bf16[2048,256]{1,0:T(8,128)(2,1)} %param.3) | copy-start | bytes 3145732
  7.2 2.3 copy-start.1
  7.2 119.0 %reduce-scatter.2.cloned.1.call-start = ((), (), s32[]{:S(2)}) async-start(), calls=%async_computation.1 | async-start | bytes 2621440 | tf_op jit(solution)/shard_map/reduce_scatter | solution.py:31
  83.9 95.0 %all-gather.3.cloned.1.call-start = ((), (), s32[]{:S(2)}) async-start(), calls=%async_computation.2 | async-start | bytes 4456448 | tf_op jit(solution)/shard_map/all_gather | solution.py:42
  181.5 60.6 %copy-start.2 = (f32[512,256]{1,0:T(8,128)S(1)}, f32[512,256]{1,0:T(8,128)}, u32[]{:S(2)}) copy-start(f32[512,256]{1,0:T(8,128)} %reduce-scatter.2.cloned.1.call-done) | copy-start | bytes 1572868
Sparse Core Ops, SparseCore 0:
  84.0 42.1 reduce-scatter.1
  129.3 49.5 all-gather.2
